TPU v7x, 32 devices: a whole 2x2x4 slice. The times are simulated.
32 devices in a mesh: grp: 2 (over y), wide: 8 (over z, x), narrow: 2 (over core).
Axes of the slice: x: 2, y: 2, z: 4, core: 2. Of those that a mesh axis runs over, the one named last changes fastest.
Arguments:
- denoised: float32 [4, 512, 512], P('grp', 'wide', 'narrow'), parts along dimension 0, may hold values from -6 to 6
- clean_volume: float32 [4, 512, 512], P('grp', 'wide', 'narrow'), parts along dimension 0, may hold values from -6 to 6
- weight: float32 [512, 512], P(('wide', 'narrow')), may hold values from 0.1 to 2
- act_in: bfloat16 [64, 4, 512, 512], P(None, 'grp', 'wide', 'narrow'), parts along dimension 1, may hold values from -6 to 6
- act_mid: bfloat16 [64, 4, 512, 512], P(None, 'grp', 'wide', 'narrow'), parts along dimension 1, as said below
- w_first: bfloat16 [27, 64, 64], replicated, may hold values from -0.15625 to 0.15625
- w_second: bfloat16 [27, 64], replicated, may hold values from -0.15625 to 0.15625
Outputs:
- grad_in: bfloat16 [64, 4, 512, 512], P(None, 'grp', 'wide', 'narrow'), parts along dimension 1
- grad_first: float32 [54, 64, 64], P('grp'), parts along dimension 0
- grad_second: float32 [54, 64], P('grp'), parts along dimension 0
There are 2 independent parts, one for each index of `grp`. A program takes and returns all parts, laid end to end along the dimension named above; an argument that names none is the same for every part. Nothing has to cross between parts.
Inputs may be any that keep to these rules, and one draw needn't show every extreme that they name: act_mid is a rectifier's output: non-negative, with many zeros.
All inputs are finite; a program needn't handle non-finite values.
Results may differ from a plain program's by a relative error of at most 0.0058.
Values may be sent and summed in bfloat16 or wider, within the bound.
No kernel may reach another device: no remote copies, remote signals or barrier semaphores. Data moves between devices by JAX's collectives and lax.ppermute only.
A program may use at most 320 MiB of HBM per device.

v0:
```python
import jax
import jax.numpy as jnp
from jax import lax
from jax.sharding import PartitionSpec as P

two_pi = 6.283185307179586
highest = lax.Precision.HIGHEST


def with_halo(x, sides, width):
    for axis, dim in sides:
        devices, length = (lax.axis_size(axis), x.shape[dim])
        up = [(i, (i + 1) % devices) for i in range(devices - 1)]
        down = [(j, i) for i, j in up]
        last = lax.slice_in_dim(x, length - width, length, axis=dim)
        first = lax.slice_in_dim(x, 0, width, axis=dim)
        before = lax.ppermute(last, axis, up)
        after = lax.ppermute(first, axis, down)
        x = jnp.concatenate([before, x, after], axis=dim)
    return x


def phase_table(left_index, right_index, length):
    product = left_index[:, None] * right_index[None, :] % length
    angles = product.astype(jnp.float32) * (two_pi / length)
    return (jnp.cos(angles), jnp.sin(angles))


def shifted_windows(padded, slices, rows_x, cols_y, taps_list):
    windows = []
    for tap_index in taps_list:
        step_z = tap_index // 9 - 1
        step_x = tap_index // 3 % 3 - 1
        step_y = tap_index % 3 - 1
        windows.append(
            padded[
                ...,
                1 - step_z : 1 - step_z + slices,
                1 - step_x : 1 - step_x + rows_x,
                1 - step_y : 1 - step_y + cols_y,
            ]
        )
    return jnp.stack(windows, axis=0)


def shards(denoised, clean_volume, weight, act_in, act_mid, w_first, w_second):
    wide_count = lax.axis_size("wide")
    narrow_count = lax.axis_size("narrow")
    slices, rows_x, half_cols = denoised.shape
    total_y = half_cols * narrow_count
    total_x = rows_x * wide_count
    kept_cols = half_cols // wide_count
    narrow_index = lax.axis_index("narrow")
    error_field = denoised - clean_volume
    columns = lax.iota(jnp.int32, total_y)
    frequency = (
        columns % half_cols // kept_cols * narrow_count + columns // half_cols
    ) * kept_cols + columns % kept_cols
    own_rows = narrow_index * half_cols + lax.iota(jnp.int32, half_cols)
    cos_y, sin_y = phase_table(own_rows, frequency, total_y)
    part_real = jnp.einsum("zxy,yc->zxc", error_field, cos_y, precision=highest)
    part_imag = -jnp.einsum("zxy,yc->zxc", error_field, sin_y, precision=highest)
    spec_real, spec_imag = (
        lax.psum_scatter(part_real, "narrow", scatter_dimension=2, tiled=True),
        lax.psum_scatter(part_imag, "narrow", scatter_dimension=2, tiled=True),
    )
    positions = lax.iota(jnp.int32, total_x)
    cos_x, sin_x = phase_table(positions, positions, total_x)
    pieces = (
        lax.all_to_all(
            spec_real.reshape(slices, rows_x, wide_count, kept_cols),
            "wide",
            split_axis=2,
            concat_axis=1,
            tiled=True,
        ),
        lax.all_to_all(
            spec_imag.reshape(slices, rows_x, wide_count, kept_cols),
            "wide",
            split_axis=2,
            concat_axis=1,
            tiled=True,
        ),
    )
    item_count = pieces[0].shape[0]
    in_real = pieces[0].reshape(item_count, total_x, kept_cols)
    in_imag = pieces[1].reshape(item_count, total_x, kept_cols)
    four_real = jnp.einsum("mxk,xq->mkq", in_real, cos_x, precision=highest) + jnp.einsum(
        "mxk,xq->mkq", in_imag, sin_x, precision=highest
    )
    four_imag = jnp.einsum("mxk,xq->mkq", in_imag, cos_x, precision=highest) - jnp.einsum(
        "mxk,xq->mkq", in_real, sin_x, precision=highest
    )
    weighted_real = weight * four_real
    weighted_imag = weight * four_imag
    out_real = jnp.einsum("mkq,qx->mxk", weighted_real, cos_x, precision=highest) - jnp.einsum(
        "mkq,qx->mxk", weighted_imag, sin_x, precision=highest
    )
    out_imag = jnp.einsum("mkq,qx->mxk", weighted_imag, cos_x, precision=highest) + jnp.einsum(
        "mkq,qx->mxk", weighted_real, sin_x, precision=highest
    )
    back_real = lax.all_to_all(
        out_real.reshape(item_count, wide_count, rows_x, kept_cols),
        "wide",
        split_axis=1,
        concat_axis=3,
        tiled=True,
    ).reshape(item_count, rows_x, half_cols)
    back_imag = lax.all_to_all(
        out_imag.reshape(item_count, wide_count, rows_x, kept_cols),
        "wide",
        split_axis=1,
        concat_axis=3,
        tiled=True,
    ).reshape(item_count, rows_x, half_cols)
    local_cols = lax.iota(jnp.int32, half_cols)
    own_freq = (
        local_cols // kept_cols * narrow_count + narrow_index
    ) * kept_cols + local_cols % kept_cols
    cos_back, sin_back = phase_table(own_freq, columns, total_y)
    part_term = jnp.einsum("zxc,cy->zxy", back_real, cos_back, precision=highest) - jnp.einsum(
        "zxc,cy->zxy", back_imag, sin_back, precision=highest
    )
    field_real = lax.psum_scatter(part_term, "narrow", scatter_dimension=2, tiled=True)
    grad_noise = (field_real * (-2.0 / (total_x * total_y))).astype(jnp.bfloat16)
    noise_rim = with_halo(grad_noise, (("wide", 1), ("narrow", 2)), 1)
    noise_pad = jnp.pad(noise_rim, ((1, 1), (0, 0), (0, 0)))
    noise_windows = shifted_windows(noise_pad, slices, rows_x, half_cols, range(27))
    grad_mid = jnp.einsum(
        "tc,tzxy->czxy", w_second, noise_windows, preferred_element_type=jnp.float32
    )
    masked = jnp.where(act_mid > 0, grad_mid, 0.0).astype(jnp.bfloat16)
    masked_rim = with_halo(masked, (("wide", 2), ("narrow", 3)), 1)
    grad_second = jnp.einsum(
        "czxy,tzxy->tc", act_mid, noise_windows, preferred_element_type=jnp.float32
    )
    masked_pad = jnp.pad(masked_rim, ((0, 0), (1, 1), (0, 0), (0, 0)))
    channels = act_in.shape[0]
    grad_in = jnp.zeros(act_in.shape, jnp.float32)
    first_parts = []
    for plane_index in range(9):
        stacked = shifted_windows(
            masked_pad, slices, rows_x, half_cols, [plane_index, plane_index + 9, plane_index + 18]
        )
        first_parts.append(
            jnp.einsum("izxy,dozxy->dio", act_in, stacked, preferred_element_type=jnp.float32)
        )
        grad_in = grad_in + jnp.einsum(
            "dio,dozxy->izxy", w_first[plane_index::9], stacked, preferred_element_type=jnp.float32
        )
    grad_first = jnp.stack(first_parts, axis=1).reshape(27, channels, channels)
    grad_first, grad_second = lax.psum((grad_first, grad_second), ("wide", "narrow"))
    return (grad_in.astype(jnp.bfloat16), grad_first, grad_second)


def solution(mesh):
    placed = (
        P("grp", "wide", "narrow"),
        P("grp", "wide", "narrow"),
        P(("wide", "narrow"), None),
        P(None, "grp", "wide", "narrow"),
        P(None, "grp", "wide", "narrow"),
        P(),
        P(),
    )
    return jax.shard_map(
        shards,
        mesh=mesh,
        in_specs=placed,
        out_specs=(P(None, "grp", "wide", "narrow"), P("grp", None, None), P("grp", None)),
        check_vma=False,
    )
```

profile of v0, /device:TPU:0, one launch (start us, length us, event | category | flops | bytes accessed | tf_op | source)
XLA Modules:
  0.0 590.2 jit_solution(6544291308981167660)
XLA Ops:
  7.3 4.1 fusion.133
  11.4 4.1 convolution_negate_fusion
  15.5 6.4 %reduce-scatter.4.cloned.1.call-done = f32[2,64,256]{2,1,0:T(8,128)} async-done(((f32[2,64,512]{2,1,0:T(8,128)}), f32[2,64,256]{2,1,0:T(8,128)}) %reduce-scatter.4.cloned.1.call-update) | async-done | bytes 131088 | tf_op jit(solution)/shard_map/reduce_scatter | solution.py:64
  23.8 5.7 all-to-all-start
  29.5 4.1 reduce-scatter.6.cloned.1.call-done
  37.0 4.8 all-to-all-start.1
  43.6 4.7 fusion.118
  50.6 4.7 fusion.114
  55.3 4.8 fusion.44
  60.1 4.8 fusion.116
  64.9 4.9 fusion.45
  69.8 4.8 fusion.112
  74.7 4.8 fusion.43
  80.5 5.2 all-to-all-start.2
  85.7 4.8 fusion.42
  93.1 4.5 all-to-all-start.3
  98.9 6.0 %all-to-all-done.3 = f32[8,1,4096]{2,1,0:T(1,128)S(1)} async-done(((f32[8,1,4096]{2,1,0:T(1,128)}), f32[8,1,4096]{2,1,0:T(1,128)S(1)}, u32[]{:S(2)}, u32[]{:S(2)}) %all-to-all-start.3) | async-done | bytes 131104 | tf_op jit(solution)/shard_map/all_to_all | solution.py:109
  106.0 2.5 fusion.130
  108.5 3.2 convolution_subtract_fusion
  111.8 5.5 reduce-scatter.8.cloned.1.call-done
  118.4 3.8 collective-permute-start
  123.5 4.2 collective-permute-done.1
  130.4 1.8 collective-permute-done.3
  135.1 4.5 fusion.7
  139.6 2.0 copy-done.2
  141.7 4.3 collective-permute-start.4
  147.6 6.3 %fusion.100 = f32[27,64]{1,0:T(8,128)S(1)} fusion(bf16[64,2,64,256]{3,2,1,0:T(8,128)(2,1)S(1)} %copy-done.27, bf16[27,2,64,256]{3,2,1,0:T(8,128)(2,1)S(1)} %constant_dynamic-update-slice_fusion), kind=kOutput, calls=%fused_computation.124 | convolution fusion | flops 113246208 | bytes 5970688 | tf_op jit(solution)/shard_map/czxy,tzxy->tc/dot_general | solution.py:134
  154.0 60.0 %psum.15 = f32[27,64]{1,0:T(8,128)} all-reduce(f32[27,64]{1,0:T(8,128)S(1)} %fusion.100), channel_id=1, replica_groups=mesh['grp'=2,'wide'=8,'narrow'=2] {'wide','narrow'}, use_global_device_ids=true, to_apply=%region_4.5 | all-reduce | flops 1728 | bytes 13824 | tf_op jit(solution)/shard_map/psum | solution.py:152
  214.0 2.5 pad_maximum_fusion.28
  216.5 2.5 fusion.284
  219.0 3.6 copy.101
  223.9 2.5 copy.102
  227.9 5.8 fusion.27
  233.7 4.5 copy.103
  238.2 4.5 copy.104
  242.7 8.2 %pad_maximum_fusion.9 = (bf16[64,2,66,257]{3,0,2,1:T(8,128)(2,1)S(1)}, bf16[64,2,66,257]{3,0,2,1:T(8,128)(2,1)S(1)}) fusion(bf16[64,2,66,1]{3,0,2,1:T(8,128)(2,1)} %copy.104, bf16[64,2,1,256]{3,0,2,1:T(8,128)(2,1)S(1)} %collective-permute-done.5, bf16[64,2,64,256]{3,0,2,1:T(8,128)(2,1)} %copy-done.2, bf16[64,2,1,256]{3,0,2,1:T(8,128)(2,1)S(1)} %collective-permute-done.4, ...), kind=kLoop, calls=%fused_computation.30 | loop fusion | flops 34738176 | bytes 13043712 | tf_op jit(solution)/shard_map/concatenate | solution.py:19
  250.9 9.2 %slice_bitcast_fusion.22 = (bf16[1,64,2,64,256]{4,1,3,2,0:T(8,128)(2,1)}, bf16[1,64,2,64,256]{4,1,3,2,0:T(8,128)(2,1)}, bf16[1,64,2,64,256]{4,1,3,2,0:T(8,128)(2,1)}) fusion(bf16[64,2,66,257]{3,0,2,1:T(8,128)(2,1)S(1)} %get-tuple-element.36), kind=kLoop, calls=%fused_computation.77 | loop fusion | bytes 25165824 | tf_op jit(solution)/shard_map/stack | solution.py:43
  260.1 8.9 %select_maximum_fusion = bf16[64,4,66,258]{3,0,2,1:T(8,128)(2,1)} fusion(bf16[64,2,66,1]{3,0,2,1:T(8,128)(2,1)} %copy.104, bf16[64,2,66,1]{3,0,2,1:T(8,128)(2,1)S(1)} %copy-done.4, bf16[64,2,1,256]{3,0,2,1:T(8,128)(2,1)S(1)} %collective-permute-done.5, bf16[64,2,64,256]{3,0,2,1:T(8,128)(2,1)S(1)} %copy-done.3, ...), kind=kLoop, calls=%fused_computation.3 | loop fusion | flops 78465024 | bytes 13077504 | tf_op jit(solution)/shard_map/concatenate | solution.py:19
  269.1 64.1 %slice_bitcast_fusion.23 = (bf16[1,64,2,64,256]{4,1,3,2,0:T(8,128)(2,1)}, bf16[1,64,2,64,256]{4,1,3,2,0:T(8,128)(2,1)}, bf16[1,64,2,64,256]{4,1,3,2,0:T(8,128)(2...) fusion(bf16[64,4,66,258]{3,0,2,1:T(8,128)(2,1)} %select_maximum, ...), kind=kLoop, calls=%fused_computation.78 | loop fusion | bytes 150994944 | tf_op jit(solution)/shard_map/stack | solution.py:43
  333.2 15.3 %fusion.49 = f32[3,9,64,64]{2,3,0,1:T(8,128)} fusion(bf16[1,64,2,64,256]{4,1,3,2,0:T(8,128)(2,1)} %get-tuple-element.28, bf16[1,64,2,64,256]{4,1,3,2,0:T(8,128)(2,1)} %get-tuple-element.30, bf16[1,64,2,64,256]{4,1,3,2,0:T(8,128)(2,1)} %get-tuple-element.12, bf16[64,2,64,256,1]{3,2,1,0,4:T(8,128)(2,1)} %bitcast.559), kind=kOutput, calls=%fused_computation.107 | convolution fusion | flops 817889280 | bytes 16875520 | tf_op jit(solution)/shard_map/izxy,dozxy->dio/dot_general | solution.py:146
  348.6 8.5 %fusion.25 = f32[2,64,256,64,1]{2,3,1,0,4:T(8,128)} fusion(bf16[1,64,2,64,256]{4,1,3,2,0:T(8,128)(2,1)} %get-tuple-element.28, bf16[1,64,2,64,256]{4,1,3,2,0:T(8,128)(2,1)} %get-tuple-element.30, bf16[1,64,2,64,256]{4,1,3,2,0:T(8,128)(2,1)} %get-tuple-element.12, bf16[27,64,64]{2,1,0:T(8,128)(2,1)S(1)} %copy-done.29), kind=kOutput, calls=%fused_computation.49 | convolution fusion | flops 843055104 | bytes 21020672 | tf_op jit(solution)/shard_map/dio,dozxy->izxy/dot_general | solution.py:148
  359.8 5.2 fusion.23
  365.0 9.2 %fusion.55 = f32[3,9,64,64]{2,3,0,1:T(8,128)} fusion(f32[3,9,64,64]{2,3,0,1:T(8,128)} %fusion.49, bf16[1,64,2,64,256]{4,1,3,2,0:T(8,128)(2,1)S(1)} %copy-done.21, bf16[1,64,2,64,256]{4,1,3,2,0:T(8,128)(2,1)S(1)} %copy-done.10, bf16[1,64,2,64,256]{4,1,3,2,0:T(8,128)(2,1)S(1)} %copy-done.22, bf16[64,2,64,256,1]{3,2,1,0,4:T(8,128)(2,1)} %bitcast.560), kind=kOutput, calls=%fused_computation.109 | convolution fusion | flops 817889280 | bytes 16875520 | tf_op jit(solution)/shard_map/izxy,dozxy->dio/dot_general | solution.py:146
  374.2 4.9 slice_bitcast_fusion.17
  379.0 2.0 copy-done.26
  381.7 5.5 fusion.21
  387.2 10.4 %fusion.61 = f32[3,9,64,64]{2,3,0,1:T(8,128)} fusion(f32[3,9,64,64]{2,3,0,1:T(8,128)} %fusion.55, bf16[1,64,2,64,256]{4,1,3,2,0:T(8,128)(2,1)S(1)} %copy-done.19, bf16[1,64,2,64,256]{4,1,3,2,0:T(8,128)(2,1)} %copy-done.26, bf16[1,64,2,64,256]{4,1,3,2,0:T(8,128)(2,1)S(1)} %copy-done.20, bf16[64,2,64,256,1]{3,2,1,0,4:T(8,128)(2,1)} %bitcast.561), kind=kOutput, calls=%fused_computation.111 | convolution fusion | flops 817889280 | bytes 16875520 | tf_op jit(solution)/shard_map/izxy,dozxy->dio/dot_general | solution.py:146
  397.6 6.5 %fusion.19 = f32[2,64,256,64,1]{2,3,1,0,4:T(8,128)} fusion(bf16[1,64,2,64,256]{4,1,3,2,0:T(8,128)(2,1)S(1)} %copy-done.17, bf16[1,64,2,64,256]{4,1,3,2,0:T(8,128)(2,1)} %get-tuple-element.32, bf16[1,64,2,64,256]{4,1,3,2,0:T(8,128)(2,1)S(1)} %copy-done.18, bf16[27,64,64]{2,1,0:T(8,128)(2,1)S(1)} %copy-done.29), kind=kOutput, calls=%fused_computation.43 | convolution fusion | flops 843055104 | bytes 21020672 | tf_op jit(solution)/shard_map/dio,dozxy->izxy/dot_general | solution.py:148
  404.2 10.4 %fusion.67 = f32[3,9,64,64]{2,3,0,1:T(8,128)} fusion(f32[3,9,64,64]{2,3,0,1:T(8,128)} %fusion.61, bf16[1,64,2,64,256]{4,1,3,2,0:T(8,128)(2,1)S(1)} %copy-done.17, bf16[1,64,2,64,256]{4,1,3,2,0:T(8,128)(2,1)} %get-tuple-element.32, bf16[1,64,2,64,256]{4,1,3,2,0:T(8,128)(2,1)S(1)} %copy-done.18, bf16[64,2,64,256,1]{3,2,1,0,4:T(8,128)(2,1)} %bitcast.562), kind=kOutput, calls=%fused_computation.113 | convolution fusion | flops 817889280 | bytes 16875520 | tf_op jit(solution)/shard_map/izxy,dozxy->dio/dot_general | solution.py:146
  414.6 5.3 fusion.17
  420.0 9.3 %fusion.73 = f32[3,9,64,64]{2,3,0,1:T(8,128)} fusion(f32[3,9,64,64]{2,3,0,1:T(8,128)} %fusion.67, bf16[1,64,2,64,256]{4,1,3,2,0:T(8,128)(2,1)S(1)} %copy-done.15, bf16[1,64,2,64,256]{4,1,3,2,0:T(8,128)(2,1)S(1)} %bitcast.549, bf16[1,64,2,64,256]{4,1,3,2,0:T(8,128)(2,1)S(1)} %copy-done.16, bf16[64,2,64,256,1]{3,2,1,0,4:T(8,128)(2,1)} %bitcast.563), kind=kOutput, calls=%fused_computation.115 | convolution fusion | flops 817889280 | bytes 16875520 | tf_op jit(solution)/shard_map/izxy,dozxy->dio/dot_general | solution.py:146
  429.3 6.6 %fusion.15 = f32[2,64,256,64,1]{2,3,1,0,4:T(8,128)} fusion(bf16[1,64,2,64,256]{4,1,3,2,0:T(8,128)(2,1)S(1)} %copy-done.13, bf16[1,64,2,64,256]{4,1,3,2,0:T(8,128)(2,1)} %get-tuple-element.35, bf16[1,64,2,64,256]{4,1,3,2,0:T(8,128)(2,1)S(1)} %copy-done.14, bf16[27,64,64]{2,1,0:T(8,128)(2,1)S(1)} %copy-done.29), kind=kOutput, calls=%fused_computation.39 | convolution fusion | flops 843055104 | bytes 21020672 | tf_op jit(solution)/shard_map/dio,dozxy->izxy/dot_general | solution.py:148
  436.0 10.4 %fusion.79 = f32[3,9,64,64]{2,3,0,1:T(8,128)} fusion(f32[3,9,64,64]{2,3,0,1:T(8,128)} %fusion.73, bf16[1,64,2,64,256]{4,1,3,2,0:T(8,128)(2,1)S(1)} %copy-done.13, bf16[1,64,2,64,256]{4,1,3,2,0:T(8,128)(2,1)} %get-tuple-element.35, bf16[1,64,2,64,256]{4,1,3,2,0:T(8,128)(2,1)S(1)} %copy-done.14, bf16[64,2,64,256,1]{3,2,1,0,4:T(8,128)(2,1)} %bitcast.564), kind=kOutput, calls=%fused_computation.117 | convolution fusion | flops 817889280 | bytes 16875520 | tf_op jit(solution)/shard_map/izxy,dozxy->dio/dot_general | solution.py:146
  446.4 5.3 fusion.13
  451.8 9.3 %fusion.85 = f32[3,9,64,64]{2,3,0,1:T(8,128)} fusion(f32[3,9,64,64]{2,3,0,1:T(8,128)} %fusion.79, bf16[1,64,2,64,256]{4,1,3,2,0:T(8,128)(2,1)S(1)} %copy-done.11, bf16[1,64,2,64,256]{4,1,3,2,0:T(8,128)(2,1)S(1)} %copy-done.24, bf16[1,64,2,64,256]{4,1,3,2,0:T(8,128)(2,1)S(1)} %copy-done.12, bf16[64,2,64,256,1]{3,2,1,0,4:T(8,128)(2,1)} %bitcast.565), kind=kOutput, calls=%fused_computation.119 | convolution fusion | flops 817889280 | bytes 16875520 | tf_op jit(solution)/shard_map/izxy,dozxy->dio/dot_general | solution.py:146
  461.2 5.5 fusion.11
  466.7 9.3 %fusion.91 = f32[3,9,64,64]{2,3,0,1:T(8,128)} fusion(f32[3,9,64,64]{2,3,0,1:T(8,128)} %fusion.85, bf16[1,64,2,64,256]{4,1,3,2,0:T(8,128)(2,1)S(1)} %copy-done.8, bf16[1,64,2,64,256]{4,1,3,2,0:T(8,128)(2,1)S(1)} %copy-done.5, bf16[1,64,2,64,256]{4,1,3,2,0:T(8,128)(2,1)S(1)} %copy-done.9, bf16[64,2,64,256,1]{3,2,1,0,4:T(8,128)(2,1)} %bitcast.566), kind=kOutput, calls=%fused_computation.121 | convolution fusion | flops 817889280 | bytes 16875520 | tf_op jit(solution)/shard_map/izxy,dozxy->dio/dot_general | solution.py:146
  476.0 5.2 fusion.9
  481.3 6.4 %fusion.97 = f32[3,9,64,64]{2,3,0,1:T(8,128)} fusion(f32[3,9,64,64]{2,3,0,1:T(8,128)} %fusion.91, bf16[1,64,2,64,256]{4,1,3,2,0:T(8,128)(2,1)S(1)} %copy-done.7, bf16[1,64,2,64,256]{4,1,3,2,0:T(8,128)(2,1)S(1)} %copy-done.25, bf16[1,64,2,64,256]{4,1,3,2,0:T(8,128)(2,1)S(1)} %copy-done.6, bf16[64,2,64,256,1]{3,2,1,0,4:T(8,128)(2,1)S(1)} %bitcast.567), kind=kOutput, calls=%fused_computation.123 | convolution fusion | flops 817889280 | bytes 16875520 | tf_op jit(solution)/shard_map/izxy,dozxy->dio/dot_general | solution.py:146
  487.7 2.4 copy.134
  490.1 25.0 %fusion.39 = bf16[64,2,64,256]{3,0,1,2:T(8,128)(2,1)S(1)} fusion(f32[2,64,256,64,1]{2,3,1,0,4:T(8,128)} %fusion.9, f32[2,64,256,64,1]{2,3,1,0,4:T(8,128)} %fusion.11, f32[2,64,256,64,1]{2,3,1,0,4:T(8,128)} %fusion.13, f32[2,64,256,64,1]{2,3,1,0,4:T(8,128)} %fusion.15, f32[2,64,256,64,1]{2,3,1,0,4:T(8,128)} %fusion.17, f32[2,64,256,64,1]{2,3,1,0,4:T(8,128)} %fusion.19, ...), kind=kLoop, calls=%fused_computation.90 | loop fusion | flops 18874368 | bytes 79691776 | tf_op jit(solution)/shard_map/convert_element_type | solution.py:153
  515.2 4.4 copy.137
  519.6 61.7 %all-reduce.4.cloned.1.call-done = f32[27,64,64]{2,1,0:T(8,128)} async-done(((f32[27,64,64]{2,1,0:T(8,128)}), f32[27,64,64]{2,1,0:T(8,128)}) %all-reduce.4.cloned.1.call-update) | async-done | bytes 442384 | tf_op jit(solution)/shard_map/psum | solution.py:152
  581.3 2.2 copy.322
  (151 shorter events, 31.2 us)
Async XLA Ops:
  7.2 128.0 %copy-start = (bf16[27,64]{1,0:T(8,128)(2,1)S(1)}, bf16[27,64]{1,0:T(8,128)(2,1)}, u32[]{:S(2)}) copy-start(bf16[27,64]{1,0:T(8,128)(2,1)} %param.13) | copy-start | bytes 10372
  7.2 14.7 %reduce-scatter.4.cloned.1.call-start = ((), (), s32[]{:S(2)}) async-start(), calls=%async_computation.7 | async-start | bytes 393216 | tf_op jit(solution)/shard_map/reduce_scatter | solution.py:64
  11.4 22.3 %reduce-scatter.6.cloned.1.call-start = ((), (), s32[]{:S(2)}) async-start(), calls=%async_computation.8 | async-start | bytes 393216 | tf_op jit(solution)/shard_map/reduce_scatter | solution.py:65
  23.8 13.2 %all-to-all-start = ((f32[8,1,4096]{2,1,0:T(1,128)}), f32[8,1,4096]{2,1,0:T(1,128)S(1)}, u32[]{:S(2)}, u32[]{:S(2)}) async-start(f32[8,1,4096]{2,1,0:T(1,128)} %reshape.165), calls=%async_computation.1 | async-start | bytes 262144 | tf_op jit(solution)/shard_map/all_to_all | solution.py:70
  37.0 12.2 %all-to-all-start.1 = ((f32[8,1,4096]{2,1,0:T(1,128)}), f32[8,1,4096]{2,1,0:T(1,128)S(1)}, u32[]{:S(2)}, u32[]{:S(2)}) async-start(f32[8,1,4096]{2,1,0:T(1,128)} %reshape.167), calls=%async_computation.3 | async-start | bytes 262144 | tf_op jit(solution)/shard_map/all_to_all | solution.py:77
  48.4 6.9 %copy-start.30 = (f32[32,512]{1,0:T(8,128)S(1)}, f32[32,512]{1,0:T(8,128)}, u32[]{:S(2)}) copy-start(f32[32,512]{1,0:T(8,128)} %param.9) | copy-start | bytes 196612
  80.5 12.6 %all-to-all-start.2 = ((f32[8,1,4096]{2,1,0:T(1,128)}), f32[8,1,4096]{2,1,0:T(1,128)S(1)}, u32[]{:S(2)}, u32[]{:S(2)}) async-start(f32[8,1,4096]{2,1,0:T(1,128)} %reshape.169), calls=%async_computation.4 | async-start | bytes 262144 | tf_op jit(solution)/shard_map/all_to_all | solution.py:102
  93.1 11.8 %all-to-all-start.3 = ((f32[8,1,4096]{2,1,0:T(1,128)}), f32[8,1,4096]{2,1,0:T(1,128)S(1)}, u32[]{:S(2)}, u32[]{:S(2)}) async-start(f32[8,1,4096]{2,1,0:T(1,128)} %reshape.171), calls=%async_computation.5 | async-start | bytes 262144 | tf_op jit(solution)/shard_map/all_to_all | solution.py:109
  97.5 19.8 %reduce-scatter.8.cloned.1.call-start = ((), (), s32[]{:S(2)}) async-start(), calls=%async_computation.9 | async-start | bytes 393216 | tf_op jit(solution)/shard_map/reduce_scatter | solution.py:124
  111.7 469.5 %all-reduce.4.cloned.1.call-start = ((), (), s32[]{:S(2)}) async-start(), calls=%async_computation.10 | async-start | bytes 1769472 | tf_op jit(solution)/shard_map/psum | solution.py:152
  117.3 17.8 %copy-start.27 = (bf16[64,2,64,256]{3,2,1,0:T(8,128)(2,1)S(1)}, bf16[64,2,64,256]{3,2,1,0:T(8,128)(2,1)}, u32[]{:S(2)}) copy-start(bf16[64,2,64,256]{3,2,1,0:T(8,128)(2,1)} %param.11) | copy-start | bytes 12582916
  118.4 5.1 collective-permute-start
  122.2 5.5 collective-permute-start.1
  127.8 2.6 collective-permute-start.2
  129.1 3.1 collective-permute-start.3
  139.6 2.0 copy-start.2
  141.7 72.4 %collective-permute-start.4 = (bf16[64,2,1,256]{3,0,2,1:T(8,128)(2,1)S(1)}, bf16[64,2,1,256]{3,0,2,1:T(8,128)(2,1)S(1)}, u32[]{:S(2)}, u32[]{:S(2)}) collective-permute-start(bf16[64,2,1,256]{3,0,2,1:T(8,128)(2,1)S(1)} %get-tuple-element.42), channel_id=1, source_target_pairs={{0,2},{2,4},{4,6},{6,8},{8,10},{10,12},{12,14},{1,3},{3,5},{5,7},{... | collective-permute-start | bytes 196616 | tf_op jit(solution)/shard_map/ppermute | solution.py:17
  145.9 68.1 %collective-permute-start.5 = (bf16[64,2,1,256]{3,0,2,1:T(8,128)(2,1)S(1)}, bf16[64,2,1,256]{3,0,2,1:T(8,128)(2,1)S(1)}, u32[]{:S(2)}, u32[]{:S(2)}) collective-permute-start(bf16[64,2,1,256]{3,0,2,1:T(8,128)(2,1)S(1)} %get-tuple-element.43), channel_id=1, source_target_pairs={{2,0},{4,2},{6,4},{8,6},{10,8},{12,10},{14,12},{3,1},{5,3},{7,5},{... | collective-permute-start | bytes 196616 | tf_op jit(solution)/shard_map/ppermute | solution.py:18
  222.6 11.1 %collective-permute-start.6 = (bf16[64,2,66,1]{2,0,3,1:T(8,128)(2,1)S(1)}, bf16[64,2,66,1]{2,0,3,1:T(8,128)(2,1)S(1)}, u32[]{:S(2)}, u32[]{:S(2)}) collective-permute-start(bf16[64,2,66,1]{2,0,3,1:T(8,128)(2,1)S(1)} %copy.101), channel_id=1, source_target_pairs={{0,1},{2,3},{4,5},{6,7},{8,9},{10,11},{12,13},{14,15},{16,17},{18,... | collective-permute-start | bytes 50696 | tf_op jit(solution)/shard_map/ppermute | solution.py:17
  226.4 11.8 %collective-permute-start.7 = (bf16[64,2,66,1]{2,0,3,1:T(8,128)(2,1)S(1)}, bf16[64,2,66,1]{2,0,3,1:T(8,128)(2,1)S(1)}, u32[]{:S(2)}, u32[]{:S(2)}) collective-permute-start(bf16[64,2,66,1]{2,0,3,1:T(8,128)(2,1)S(1)} %copy.102), channel_id=1, source_target_pairs={{1,0},{3,2},{5,4},{7,6},{9,8},{11,10},{13,12},{15,14},{17,16},{19,... | collective-permute-start | bytes 50696 | tf_op jit(solution)/shard_map/ppermute | solution.py:18
  250.9 9.2 %copy-start.3 = (bf16[64,2,64,256]{3,0,2,1:T(8,128)(2,1)S(1)}, bf16[64,2,64,256]{3,0,2,1:T(8,128)(2,1)}, u32[]{:S(2)}) copy-start(bf16[64,2,64,256]{3,0,2,1:T(8,128)(2,1)} %copy-done.2) | copy-start | bytes 12582916
  250.9 9.2 %copy-start.4 = (bf16[64,2,66,1]{3,0,2,1:T(8,128)(2,1)S(1)}, bf16[64,2,66,1]{3,0,2,1:T(8,128)(2,1)}, u32[]{:S(2)}) copy-start(bf16[64,2,66,1]{3,0,2,1:T(8,128)(2,1)} %copy.103) | copy-start | bytes 50692
  333.2 15.4 %copy-start.29 = (bf16[27,64,64]{2,1,0:T(8,128)(2,1)S(1)}, bf16[27,64,64]{2,1,0:T(8,128)(2,1)}, u32[]{:S(2)}) copy-start(bf16[27,64,64]{2,1,0:T(8,128)(2,1)} %param.12) | copy-start | bytes 663556
  348.6 8.5 %copy-start.10 = (bf16[1,64,2,64,256]{4,1,3,2,0:T(8,128)(2,1)S(1)}, bf16[1,64,2,64,256]{4,1,3,2,0:T(8,128)(2,1)}, u32[]{:S(2)}) copy-start(bf16[1,64,2,64,256]{4,1,3,2,0:T(8,128)(2,1)} %get-tuple-element.40) | copy-start | bytes 12582916
  348.6 10.0 %copy-start.21 = (bf16[1,64,2,64,256]{4,1,3,2,0:T(8,128)(2,1)S(1)}, bf16[1,64,2,64,256]{4,1,3,2,0:T(8,128)(2,1)}, u32[]{:S(2)}) copy-start(bf16[1,64,2,64,256]{4,1,3,2,0:T(8,128)(2,1)} %get-tuple-element.26) | copy-start | bytes 12582916
  348.6 11.2 %copy-start.22 = (bf16[1,64,2,64,256]{4,1,3,2,0:T(8,128)(2,1)S(1)}, bf16[1,64,2,64,256]{4,1,3,2,0:T(8,128)(2,1)}, u32[]{:S(2)}) copy-start(bf16[1,64,2,64,256]{4,1,3,2,0:T(8,128)(2,1)} %get-tuple-element.27) | copy-start | bytes 12582916
  374.2 6.9 %copy-start.19 = (bf16[1,64,2,64,256]{4,1,3,2,0:T(8,128)(2,1)S(1)}, bf16[1,64,2,64,256]{4,1,3,2,0:T(8,128)(2,1)}, u32[]{:S(2)}) copy-start(bf16[1,64,2,64,256]{4,1,3,2,0:T(8,128)(2,1)} %get-tuple-element.24) | copy-start | bytes 12582916
  374.2 7.6 %copy-start.20 = (bf16[1,64,2,64,256]{4,1,3,2,0:T(8,128)(2,1)S(1)}, bf16[1,64,2,64,256]{4,1,3,2,0:T(8,128)(2,1)}, u32[]{:S(2)}) copy-start(bf16[1,64,2,64,256]{4,1,3,2,0:T(8,128)(2,1)} %get-tuple-element.25) | copy-start | bytes 12582916
  379.0 2.0 copy-start.26
  387.2 10.4 %copy-start.17 = (bf16[1,64,2,64,256]{4,1,3,2,0:T(8,128)(2,1)S(1)}, bf16[1,64,2,64,256]{4,1,3,2,0:T(8,128)(2,1)}, u32[]{:S(2)}) copy-start(bf16[1,64,2,64,256]{4,1,3,2,0:T(8,128)(2,1)} %get-tuple-element.22) | copy-start | bytes 12582916
  387.2 10.4 %copy-start.18 = (bf16[1,64,2,64,256]{4,1,3,2,0:T(8,128)(2,1)S(1)}, bf16[1,64,2,64,256]{4,1,3,2,0:T(8,128)(2,1)}, u32[]{:S(2)}) copy-start(bf16[1,64,2,64,256]{4,1,3,2,0:T(8,128)(2,1)} %get-tuple-element.23) | copy-start | bytes 12582916
  404.2 10.4 %copy-start.15 = (bf16[1,64,2,64,256]{4,1,3,2,0:T(8,128)(2,1)S(1)}, bf16[1,64,2,64,256]{4,1,3,2,0:T(8,128)(2,1)}, u32[]{:S(2)}) copy-start(bf16[1,64,2,64,256]{4,1,3,2,0:T(8,128)(2,1)} %get-tuple-element.20) | copy-start | bytes 12582916
  404.2 10.4 %copy-start.16 = (bf16[1,64,2,64,256]{4,1,3,2,0:T(8,128)(2,1)S(1)}, bf16[1,64,2,64,256]{4,1,3,2,0:T(8,128)(2,1)}, u32[]{:S(2)}) copy-start(bf16[1,64,2,64,256]{4,1,3,2,0:T(8,128)(2,1)} %get-tuple-element.21) | copy-start | bytes 12582916
  419.9 9.4 %copy-start.13 = (bf16[1,64,2,64,256]{4,1,3,2,0:T(8,128)(2,1)S(1)}, bf16[1,64,2,64,256]{4,1,3,2,0:T(8,128)(2,1)}, u32[]{:S(2)}) copy-start(bf16[1,64,2,64,256]{4,1,3,2,0:T(8,128)(2,1)} %get-tuple-element.18) | copy-start | bytes 12582916
  420.0 9.4 %copy-start.14 = (bf16[1,64,2,64,256]{4,1,3,2,0:T(8,128)(2,1)S(1)}, bf16[1,64,2,64,256]{4,1,3,2,0:T(8,128)(2,1)}, u32[]{:S(2)}) copy-start(bf16[1,64,2,64,256]{4,1,3,2,0:T(8,128)(2,1)} %get-tuple-element.19) | copy-start | bytes 12582916
  435.9 10.5 %copy-start.11 = (bf16[1,64,2,64,256]{4,1,3,2,0:T(8,128)(2,1)S(1)}, bf16[1,64,2,64,256]{4,1,3,2,0:T(8,128)(2,1)}, u32[]{:S(2)}) copy-start(bf16[1,64,2,64,256]{4,1,3,2,0:T(8,128)(2,1)} %get-tuple-element.16) | copy-start | bytes 12582916
  436.0 10.4 %copy-start.12 = (bf16[1,64,2,64,256]{4,1,3,2,0:T(8,128)(2,1)S(1)}, bf16[1,64,2,64,256]{4,1,3,2,0:T(8,128)(2,1)}, u32[]{:S(2)}) copy-start(bf16[1,64,2,64,256]{4,1,3,2,0:T(8,128)(2,1)} %get-tuple-element.17) | copy-start | bytes 12582916
  436.0 10.4 %copy-start.23 = (bf16[1,64,2,64,256]{4,1,3,2,0:T(8,128)(2,1)S(1)}, bf16[1,64,2,64,256]{4,1,3,2,0:T(8,128)(2,1)}, u32[]{:S(2)}) copy-start(bf16[1,64,2,64,256]{4,1,3,2,0:T(8,128)(2,1)} %get-tuple-element.31) | copy-start | bytes 12582916
  446.4 5.3 copy-start.24
  451.8 9.4 %copy-start.5 = (bf16[1,64,2,64,256]{4,1,3,2,0:T(8,128)(2,1)S(1)}, bf16[1,64,2,64,256]{4,1,3,2,0:T(8,128)(2,1)}, u32[]{:S(2)}) copy-start(bf16[1,64,2,64,256]{4,1,3,2,0:T(8,128)(2,1)} %get-tuple-element.41) | copy-start | bytes 12582916
  451.8 9.4 %copy-start.8 = (bf16[1,64,2,64,256]{4,1,3,2,0:T(8,128)(2,1)S(1)}, bf16[1,64,2,64,256]{4,1,3,2,0:T(8,128)(2,1)}, u32[]{:S(2)}) copy-start(bf16[1,64,2,64,256]{4,1,3,2,0:T(8,128)(2,1)} %get-tuple-element.14) | copy-start | bytes 12582916
  451.8 9.4 %copy-start.9 = (bf16[1,64,2,64,256]{4,1,3,2,0:T(8,128)(2,1)S(1)}, bf16[1,64,2,64,256]{4,1,3,2,0:T(8,128)(2,1)}, u32[]{:S(2)}) copy-start(bf16[1,64,2,64,256]{4,1,3,2,0:T(8,128)(2,1)} %get-tuple-element.15) | copy-start | bytes 12582916
  466.6 9.4 %copy-start.6 = (bf16[1,64,2,64,256]{4,1,3,2,0:T(8,128)(2,1)S(1)}, bf16[1,64,2,64,256]{4,1,3,2,0:T(8,128)(2,1)}, u32[]{:S(2)}) copy-start(bf16[1,64,2,64,256]{4,1,3,2,0:T(8,128)(2,1)} %get-tuple-element.13) | copy-start | bytes 12582916
  466.6 9.4 %copy-start.7 = (bf16[1,64,2,64,256]{4,1,3,2,0:T(8,128)(2,1)S(1)}, bf16[1,64,2,64,256]{4,1,3,2,0:T(8,128)(2,1)}, u32[]{:S(2)}) copy-start(bf16[1,64,2,64,256]{4,1,3,2,0:T(8,128)(2,1)} %get-tuple-element.29) | copy-start | bytes 12582916
  466.7 9.4 %copy-start.25 = (bf16[1,64,2,64,256]{4,1,3,2,0:T(8,128)(2,1)S(1)}, bf16[1,64,2,64,256]{4,1,3,2,0:T(8,128)(2,1)}, u32[]{:S(2)}) copy-start(bf16[1,64,2,64,256]{4,1,3,2,0:T(8,128)(2,1)} %get-tuple-element.34) | copy-start | bytes 12582916
  476.0 5.2 copy-start.28
  490.1 93.3 %copy-start.1 = (bf16[27,64]{1,0:T(8,128)(2,1)S(1)}, bf16[27,64]{1,0:T(8,128)(2,1)}, u32[]{:S(2)}) copy-start(bf16[27,64]{1,0:T(8,128)(2,1)} %param.13) | copy-start | bytes 10372
Sparse Core Ops, SparseCore 0:
  11.5 10.3 reduce-scatter.3
  24.8 8.8 reduce-scatter.5
  111.9 5.4 reduce-scatter.7
  490.3 90.9 all-reduce.3
where the time goes:
time: 596 us; the launch traced here: 590 us
  matrix products  207 us (35%)
  local copies, waits for them, and re-layouts  121 us (20%)
  waiting for transfers between devices  93.5 us (16%)
  blocking collectives  60 us (10%)
  other arithmetic  56.7 us (10%)
  starting transfers between devices  36.9 us (6%)
  between operations  14.8 us (2%)
    dot_general x9, matrix products, shards(): jnp.einsum('izxy,dozxy->dio', act_in, stacked, preferred_element_type=jnp...  90.2 us
    another operation x4, local copies, waits for them, and re-layouts, shifted_windows(): return jnp.stack(windows, axis=0)  78.2 us
    psum x1, waiting for transfers between devices, shards(): lax.psum((grad_first, grad_second), ('wide', 'narrow'))  61.7 us
    psum x1, blocking collectives, shards(): lax.psum((grad_first, grad_second), ('wide', 'narrow'))  60 us
    dot_general x9, matrix products, shards(): jnp.einsum('dio,dozxy->izxy', w_first[plane_index::9], stacked, preferred...  53.7 us
    convert_element_type x1, other arithmetic, shards(): return (grad_in.astype(jnp.bfloat16), grad_first, grad_second)  25 us
    concatenate x6, other arithmetic, with_halo(): x = jnp.concatenate([before, x, after], axis=dim)  19.9 us
    unnamed x95, local copies, waits for them, and re-layouts  19.5 us
  transfers between devices with their start and end apart: 16, of which 10 were waited for; matrix products, arithmetic and copies ran while one was open for 12% of the time, Pallas kernels for 0%

commit v1 on v0

--- a/solution.py
+++ b/solution.py
@@ -2,6 +2,7 @@
 import jax.numpy as jnp
 from jax import lax
 from jax.sharding import PartitionSpec as P
+from jax.lax import psum
 
 two_pi = 6.283185307179586
 highest = lax.Precision.HIGHEST
@@ -44,6 +45,12 @@
 
 
 def shards(denoised, clean_volume, weight, act_in, act_mid, w_first, w_second):
+
+    def _recast_map(x0, ax_name, named_axis):
+        for s in (ax_name, named_axis):
+            x0 = psum(x0, s)
+        return x0
+
     wide_count = lax.axis_size("wide")
     narrow_count = lax.axis_size("narrow")
     slices, rows_x, half_cols = denoised.shape
@@ -149,7 +156,7 @@
             "dio,dozxy->izxy", w_first[plane_index::9], stacked, preferred_element_type=jnp.float32
         )
     grad_first = jnp.stack(first_parts, axis=1).reshape(27, channels, channels)
-    grad_first, grad_second = lax.psum((grad_first, grad_second), ("wide", "narrow"))
+    grad_first, grad_second = _recast_map((grad_first, grad_second), "narrow", "wide")
     return (grad_in.astype(jnp.bfloat16), grad_first, grad_second)
 
 

time: 596 us -> 584 us (0.980)
  blocking collectives: 60 us -> 39.8 us
  matrix products: 207 us -> 216 us
    psum x1 -> x2, blocking collectives: 60 us -> 39.8 us  [_recast_map(): x0 = psum(x0, s)]
    psum x1 -> x2, waiting for transfers between devices: 61.7 us -> 60.2 us  [_recast_map(): x0 = psum(x0, s)]
  transfers between devices with their start and end apart: 16 -> 17, of which waited for: 10 -> 11; matrix products, arithmetic and copies ran while one was open for 12% -> 14% of each run, Pallas kernels for 0% -> 0%
where the time goes in v1:
time: 584 us; the launch traced here: 579 us
  matrix products  216 us (37%)
  local copies, waits for them, and re-layouts  122 us (21%)
  waiting for transfers between devices  92.1 us (16%)
  other arithmetic  56.7 us (10%)
  blocking collectives  39.8 us (7%)
  starting transfers between devices  36.8 us (6%)
  between operations  14.9 us (3%)
    dot_general x9, matrix products, shards(): jnp.einsum('izxy,dozxy->dio', act_in, stacked, preferred_element_type=jnp...  96.1 us
    another operation x4, local copies, waits for them, and re-layouts, shifted_windows(): return jnp.stack(windows, axis=0)  78.2 us
    psum x2, waiting for transfers between devices, _recast_map(): x0 = psum(x0, s)  60.2 us
    dot_general x9, matrix products, shards(): jnp.einsum('dio,dozxy->izxy', w_first[plane_index::9], stacked, preferred...  56.7 us
    psum x2, blocking collectives, _recast_map(): x0 = psum(x0, s)  39.8 us
    convert_element_type x1, other arithmetic, shards(): return (grad_in.astype(jnp.bfloat16), grad_first, grad_second)  25.1 us
    unnamed x95, local copies, waits for them, and re-layouts  20.2 us
    concatenate x6, other arithmetic, with_halo(): x = jnp.concatenate([before, x, after], axis=dim)  19.9 us
  transfers between devices with their start and end apart: 17, of which 11 were waited for; matrix products, arithmetic and copies ran while one was open for 14% of the time, Pallas kernels for 0%

profile of v1, /device:TPU:0, one launch (start us, length us, event | category | flops | bytes accessed | tf_op | source)
XLA Modules:
  0.0 578.8 jit_solution(2518009259612662557)
XLA Ops:
  7.3 4.1 fusion.133
  11.4 4.1 convolution_negate_fusion
  15.5 6.4 %reduce-scatter.4.cloned.1.call-done = f32[2,64,256]{2,1,0:T(8,128)} async-done(((f32[2,64,512]{2,1,0:T(8,128)}), f32[2,64,256]{2,1,0:T(8,128)}) %reduce-scatter.4.cloned.1.call-update) | async-done | bytes 131088 | tf_op jit(solution)/shard_map/reduce_scatter | solution.py:71
  23.8 5.7 all-to-all-start
  29.5 4.1 reduce-scatter.6.cloned.1.call-done
  37.0 4.6 all-to-all-start.1
  43.5 4.7 fusion.118
  50.4 4.7 fusion.114
  55.1 4.8 fusion.44
  59.9 4.8 fusion.116
  64.7 5.3 fusion.45
  70.0 4.8 fusion.112
  74.8 4.8 fusion.43
  80.7 5.2 all-to-all-start.2
  85.9 4.8 fusion.42
  93.2 4.5 all-to-all-start.3
  99.1 6.0 %all-to-all-done.3 = f32[8,1,4096]{2,1,0:T(1,128)S(1)} async-done(((f32[8,1,4096]{2,1,0:T(1,128)}), f32[8,1,4096]{2,1,0:T(1,128)S(1)}, u32[]{:S(2)}, u32[]{:S(2)}) %all-to-all-start.3) | async-done | bytes 131104 | tf_op jit(solution)/shard_map/all_to_all | solution.py:116
  106.2 2.5 fusion.130
  108.7 3.2 convolution_subtract_fusion
  112.0 5.5 reduce-scatter.8.cloned.1.call-done
  118.6 3.7 collective-permute-start
  123.7 4.2 collective-permute-done.1
  135.3 4.5 fusion.7
  141.8 4.3 collective-permute-start.4
  147.6 6.3 %fusion.100 = f32[27,64]{1,0:T(8,128)S(1)} fusion(bf16[64,2,64,256]{3,2,1,0:T(8,128)(2,1)S(1)} %copy-done.28, bf16[27,2,64,256]{3,2,1,0:T(8,128)(2,1)S(1)} %constant_dynamic-update-slice_fusion), kind=kOutput, calls=%fused_computation.124 | convolution fusion | flops 113246208 | bytes 5970688 | tf_op jit(solution)/shard_map/czxy,tzxy->tc/dot_general | solution.py:141
  154.0 3.4 psum.30
  157.3 36.5 %psum.31 = f32[27,64]{1,0:T(8,128)} all-reduce(f32[27,64]{1,0:T(8,128)S(1)} %psum.30), channel_id=1, replica_groups=mesh['grp'=2,'wide'=8,'narrow'=2] {'wide'}, use_global_device_ids=true, to_apply=%region_6.7 | all-reduce | flops 1728 | bytes 13824 | tf_op jit(solution)/shard_map/psum | solution.py:51
  193.8 2.5 pad_maximum_fusion.28
  196.3 2.5 fusion.284
  198.8 3.6 copy.101
  203.7 2.5 copy.102
  207.9 5.8 %fusion.27 = (bf16[1,64,2,64,256]{4,1,3,2,0:T(8,128)(2,1)}, bf16[1,64,2,64,256]{4,1,3,2,0:T(8,128)(2,1)}) fusion(bf16[64,2,1,256]{3,0,2,1:T(8,128)(2,1)S(1)} %collective-permute-done.5, bf16[64,2,64,256]{3,0,2,1:T(8,128)(2,1)} %copy-done.2, bf16[64,2,1,256]{3,0,2,1:T(8,128)(2,1)S(1)} %collective-permute-done.4), kind=kLoop, calls=%fused_computation.74 | loop fusion | flops 4194304 | bytes 12713984 | tf_op jit(solution)/shard_map/stack | solution.py:44
  213.8 4.5 copy.103
  218.2 4.5 copy.104
  222.7 8.2 %pad_maximum_fusion.9 = (bf16[64,2,66,257]{3,0,2,1:T(8,128)(2,1)S(1)}, bf16[64,2,66,257]{3,0,2,1:T(8,128)(2,1)S(1)}) fusion(bf16[64,2,66,1]{3,0,2,1:T(8,128)(2,1)} %copy.104, bf16[64,2,1,256]{3,0,2,1:T(8,128)(2,1)S(1)} %collective-permute-done.5, bf16[64,2,64,256]{3,0,2,1:T(8,128)(2,1)} %copy-done.2, bf16[64,2,1,256]{3,0,2,1:T(8,128)(2,1)S(1)} %collective-permute-done.4, ...), kind=kLoop, calls=%fused_computation.30 | loop fusion | flops 34738176 | bytes 13043712 | tf_op jit(solution)/shard_map/concatenate | solution.py:20
  230.9 9.2 %slice_bitcast_fusion.22 = (bf16[1,64,2,64,256]{4,1,3,2,0:T(8,128)(2,1)}, bf16[1,64,2,64,256]{4,1,3,2,0:T(8,128)(2,1)}, bf16[1,64,2,64,256]{4,1,3,2,0:T(8,128)(2,1)}) fusion(bf16[64,2,66,257]{3,0,2,1:T(8,128)(2,1)S(1)} %get-tuple-element.36), kind=kLoop, calls=%fused_computation.77 | loop fusion | bytes 25165824 | tf_op jit(solution)/shard_map/stack | solution.py:44
  240.1 9.0 %select_maximum_fusion = bf16[64,4,66,258]{3,0,2,1:T(8,128)(2,1)} fusion(bf16[64,2,66,1]{3,0,2,1:T(8,128)(2,1)} %copy.104, bf16[64,2,66,1]{3,0,2,1:T(8,128)(2,1)S(1)} %copy-done.4, bf16[64,2,1,256]{3,0,2,1:T(8,128)(2,1)S(1)} %collective-permute-done.5, bf16[64,2,64,256]{3,0,2,1:T(8,128)(2,1)S(1)} %copy-done.3, ...), kind=kLoop, calls=%fused_computation.3 | loop fusion | flops 78465024 | bytes 13077504 | tf_op jit(solution)/shard_map/concatenate | solution.py:20
  249.0 64.1 %slice_bitcast_fusion.23 = (bf16[1,64,2,64,256]{4,1,3,2,0:T(8,128)(2,1)}, bf16[1,64,2,64,256]{4,1,3,2,0:T(8,128)(2,1)}, bf16[1,64,2,64,256]{4,1,3,2,0:T(8,128)(2...) fusion(bf16[64,4,66,258]{3,0,2,1:T(8,128)(2,1)} %select_maximum, ...), kind=kLoop, calls=%fused_computation.78 | loop fusion | bytes 150994944 | tf_op jit(solution)/shard_map/stack | solution.py:44
  313.1 14.6 %fusion.49 = f32[3,9,64,64]{2,3,0,1:T(8,128)S(1)} fusion(bf16[1,64,2,64,256]{4,1,3,2,0:T(8,128)(2,1)} %get-tuple-element.28, bf16[1,64,2,64,256]{4,1,3,2,0:T(8,128)(2,1)} %get-tuple-element.30, bf16[1,64,2,64,256]{4,1,3,2,0:T(8,128)(2,1)} %get-tuple-element.12, bf16[64,2,64,256,1]{3,2,1,0,4:T(8,128)(2,1)} %bitcast.559), kind=kOutput, calls=%fused_computation.107 | convolution fusion | flops 817889280 | bytes 16875520 | tf_op jit(solution)/shard_map/izxy,dozxy->dio/dot_general | solution.py:153
  327.8 8.5 %fusion.25 = f32[2,64,256,64,1]{2,3,1,0,4:T(8,128)} fusion(bf16[1,64,2,64,256]{4,1,3,2,0:T(8,128)(2,1)} %get-tuple-element.28, bf16[1,64,2,64,256]{4,1,3,2,0:T(8,128)(2,1)} %get-tuple-element.30, bf16[1,64,2,64,256]{4,1,3,2,0:T(8,128)(2,1)} %get-tuple-element.12, bf16[27,64,64]{2,1,0:T(8,128)(2,1)S(1)} %copy-done.29), kind=kOutput, calls=%fused_computation.49 | convolution fusion | flops 843055104 | bytes 21020672 | tf_op jit(solution)/shard_map/dio,dozxy->izxy/dot_general | solution.py:155
  339.0 5.2 fusion.23
  344.1 10.0 %fusion.55 = f32[3,9,64,64]{2,3,0,1:T(8,128)S(1)} fusion(f32[3,9,64,64]{2,3,0,1:T(8,128)S(1)} %fusion.49, bf16[1,64,2,64,256]{4,1,3,2,0:T(8,128)(2,1)S(1)} %copy-done.21, bf16[1,64,2,64,256]{4,1,3,2,0:T(8,128)(2,1)S(1)} %copy-done.10, bf16[1,64,2,64,256]{4,1,3,2,0:T(8,128)(2,1)S(1)} %copy-done.22, bf16[64,2,64,256,1]{3,2,1,0,4:T(8,128)(2,1)} %bitcast.560), kind=kOutput, calls=%fused_computation.109 | convolution fusion | flops 817889280 | bytes 16875520 | tf_op jit(solution)/shard_map/izxy,dozxy->dio/dot_general | solution.py:153
  354.2 4.9 slice_bitcast_fusion.17
  359.1 2.0 copy-done.26
  361.6 5.3 fusion.21
  366.9 11.4 %fusion.61 = f32[3,9,64,64]{2,3,0,1:T(8,128)S(1)} fusion(f32[3,9,64,64]{2,3,0,1:T(8,128)S(1)} %fusion.55, bf16[1,64,2,64,256]{4,1,3,2,0:T(8,128)(2,1)S(1)} %copy-done.19, bf16[1,64,2,64,256]{4,1,3,2,0:T(8,128)(2,1)} %copy-done.26, bf16[1,64,2,64,256]{4,1,3,2,0:T(8,128)(2,1)S(1)} %copy-done.20, bf16[64,2,64,256,1]{3,2,1,0,4:T(8,128)(2,1)} %bitcast.561), kind=kOutput, calls=%fused_computation.111 | convolution fusion | flops 817889280 | bytes 16875520 | tf_op jit(solution)/shard_map/izxy,dozxy->dio/dot_general | solution.py:153
  378.3 6.8 %fusion.19 = f32[2,64,256,64,1]{2,3,1,0,4:T(8,128)} fusion(bf16[1,64,2,64,256]{4,1,3,2,0:T(8,128)(2,1)S(1)} %copy-done.17, bf16[1,64,2,64,256]{4,1,3,2,0:T(8,128)(2,1)} %get-tuple-element.32, bf16[1,64,2,64,256]{4,1,3,2,0:T(8,128)(2,1)S(1)} %copy-done.18, bf16[27,64,64]{2,1,0:T(8,128)(2,1)S(1)} %copy-done.29), kind=kOutput, calls=%fused_computation.43 | convolution fusion | flops 843055104 | bytes 21020672 | tf_op jit(solution)/shard_map/dio,dozxy->izxy/dot_general | solution.py:155
  385.2 11.5 %fusion.67 = f32[3,9,64,64]{2,3,0,1:T(8,128)S(1)} fusion(f32[3,9,64,64]{2,3,0,1:T(8,128)S(1)} %fusion.61, bf16[1,64,2,64,256]{4,1,3,2,0:T(8,128)(2,1)S(1)} %copy-done.17, bf16[1,64,2,64,256]{4,1,3,2,0:T(8,128)(2,1)} %get-tuple-element.32, bf16[1,64,2,64,256]{4,1,3,2,0:T(8,128)(2,1)S(1)} %copy-done.18, bf16[64,2,64,256,1]{3,2,1,0,4:T(8,128)(2,1)} %bitcast.562), kind=kOutput, calls=%fused_computation.113 | convolution fusion | flops 817889280 | bytes 16875520 | tf_op jit(solution)/shard_map/izxy,dozxy->dio/dot_general | solution.py:153
  396.7 5.3 fusion.17
  402.0 10.3 %fusion.73 = f32[3,9,64,64]{2,3,0,1:T(8,128)S(1)} fusion(f32[3,9,64,64]{2,3,0,1:T(8,128)S(1)} %fusion.67, bf16[1,64,2,64,256]{4,1,3,2,0:T(8,128)(2,1)S(1)} %copy-done.15, bf16[1,64,2,64,256]{4,1,3,2,0:T(8,128)(2,1)S(1)} %bitcast.549, bf16[1,64,2,64,256]{4,1,3,2,0:T(8,128)(2,1)S(1)} %copy-done.16, bf16[64,2,64,256,1]{3,2,1,0,4:T(8,128)(2,1)} %bitcast.563), kind=kOutput, calls=%fused_computation.115 | convolution fusion | flops 817889280 | bytes 16875520 | tf_op jit(solution)/shard_map/izxy,dozxy->dio/dot_general | solution.py:153
  413.3 6.6 %fusion.15 = f32[2,64,256,64,1]{2,3,1,0,4:T(8,128)} fusion(bf16[1,64,2,64,256]{4,1,3,2,0:T(8,128)(2,1)S(1)} %copy-done.13, bf16[1,64,2,64,256]{4,1,3,2,0:T(8,128)(2,1)} %get-tuple-element.35, bf16[1,64,2,64,256]{4,1,3,2,0:T(8,128)(2,1)S(1)} %copy-done.14, bf16[27,64,64]{2,1,0:T(8,128)(2,1)S(1)} %copy-done.29), kind=kOutput, calls=%fused_computation.39 | convolution fusion | flops 843055104 | bytes 21020672 | tf_op jit(solution)/shard_map/dio,dozxy->izxy/dot_general | solution.py:155
  419.9 10.4 %fusion.79 = f32[3,9,64,64]{2,3,0,1:T(8,128)} fusion(f32[3,9,64,64]{2,3,0,1:T(8,128)} %copy-done.27, bf16[1,64,2,64,256]{4,1,3,2,0:T(8,128)(2,1)S(1)} %copy-done.13, bf16[1,64,2,64,256]{4,1,3,2,0:T(8,128)(2,1)} %get-tuple-element.35, bf16[1,64,2,64,256]{4,1,3,2,0:T(8,128)(2,1)S(1)} %copy-done.14, bf16[64,2,64,256,1]{3,2,1,0,4:T(8,128)(2,1)} %bitcast.564), kind=kOutput, calls=%fused_computation.117 | convolution fusion | flops 817889280 | bytes 16875520 | tf_op jit(solution)/shard_map/izxy,dozxy->dio/dot_general | solution.py:153
  430.3 5.3 fusion.13
  435.7 9.3 %fusion.85 = f32[3,9,64,64]{2,3,0,1:T(8,128)} fusion(f32[3,9,64,64]{2,3,0,1:T(8,128)} %fusion.79, bf16[1,64,2,64,256]{4,1,3,2,0:T(8,128)(2,1)S(1)} %copy-done.11, bf16[1,64,2,64,256]{4,1,3,2,0:T(8,128)(2,1)S(1)} %copy-done.24, bf16[1,64,2,64,256]{4,1,3,2,0:T(8,128)(2,1)S(1)} %copy-done.12, bf16[64,2,64,256,1]{3,2,1,0,4:T(8,128)(2,1)} %bitcast.565), kind=kOutput, calls=%fused_computation.119 | convolution fusion | flops 817889280 | bytes 16875520 | tf_op jit(solution)/shard_map/izxy,dozxy->dio/dot_general | solution.py:153
  445.0 5.4 fusion.11
  450.5 9.3 %fusion.91 = f32[3,9,64,64]{2,3,0,1:T(8,128)} fusion(f32[3,9,64,64]{2,3,0,1:T(8,128)} %fusion.85, bf16[1,64,2,64,256]{4,1,3,2,0:T(8,128)(2,1)S(1)} %copy-done.8, bf16[1,64,2,64,256]{4,1,3,2,0:T(8,128)(2,1)S(1)} %copy-done.5, bf16[1,64,2,64,256]{4,1,3,2,0:T(8,128)(2,1)S(1)} %copy-done.9, bf16[64,2,64,256,1]{3,2,1,0,4:T(8,128)(2,1)} %bitcast.566), kind=kOutput, calls=%fused_computation.121 | convolution fusion | flops 817889280 | bytes 16875520 | tf_op jit(solution)/shard_map/izxy,dozxy->dio/dot_general | solution.py:153
  459.9 9.2 %fusion.97 = f32[3,9,64,64]{2,3,0,1:T(8,128)} fusion(f32[3,9,64,64]{2,3,0,1:T(8,128)} %fusion.91, bf16[1,64,2,64,256]{4,1,3,2,0:T(8,128)(2,1)S(1)} %copy-done.7, bf16[1,64,2,64,256]{4,1,3,2,0:T(8,128)(2,1)S(1)} %copy-done.25, bf16[1,64,2,64,256]{4,1,3,2,0:T(8,128)(2,1)S(1)} %copy-done.6, bf16[64,2,64,256,1]{3,2,1,0,4:T(8,128)(2,1)} %bitcast.567), kind=kOutput, calls=%fused_computation.123 | convolution fusion | flops 817889280 | bytes 16875520 | tf_op jit(solution)/shard_map/izxy,dozxy->dio/dot_general | solution.py:153
  469.1 2.6 copy.134
  471.7 8.4 %fusion.9 = f32[2,64,256,64,1]{2,3,1,0,4:T(8,128)} fusion(bf16[1,64,2,64,256]{4,1,3,2,0:T(8,128)(2,1)} %get-tuple-element.29, bf16[1,64,2,64,256]{4,1,3,2,0:T(8,128)(2,1)} %get-tuple-element.34, bf16[1,64,2,64,256]{4,1,3,2,0:T(8,128)(2,1)} %get-tuple-element.13, bf16[27,64,64]{2,1,0:T(8,128)(2,1)S(1)} %copy-done.29), kind=kOutput, calls=%fused_computation.33 | convolution fusion | flops 843055104 | bytes 21020672 | tf_op jit(solution)/shard_map/dio,dozxy->izxy/dot_general | solution.py:155
  480.1 9.1 %all-reduce.5.cloned.1.call-done = f32[27,64,64]{2,1,0:T(8,128)} async-done(((f32[27,64,64]{2,1,0:T(8,128)}), f32[27,64,64]{2,1,0:T(8,128)}) %all-reduce.5.cloned.1.call-update) | async-done | bytes 442384 | tf_op jit(solution)/shard_map/psum | solution.py:51
  489.2 25.1 %fusion.39 = bf16[64,2,64,256]{3,0,1,2:T(8,128)(2,1)S(1)} fusion(f32[2,64,256,64,1]{2,3,1,0,4:T(8,128)} %fusion.9, f32[2,64,256,64,1]{2,3,1,0,4:T(8,128)} %fusion.11, f32[2,64,256,64,1]{2,3,1,0,4:T(8,128)} %fusion.13, f32[2,64,256,64,1]{2,3,1,0,4:T(8,128)} %fusion.15, f32[2,64,256,64,1]{2,3,1,0,4:T(8,128)} %fusion.17, f32[2,64,256,64,1]{2,3,1,0,4:T(8,128)} %fusion.19, ...), kind=kLoop, calls=%fused_computation.90 | loop fusion | flops 18874368 | bytes 79691776 | tf_op jit(solution)/shard_map/convert_element_type | solution.py:160
  514.3 4.4 copy.137
  518.7 51.2 %all-reduce.7.cloned.1.call-done = f32[27,64,64]{2,1,0:T(8,128)} async-done(((f32[27,64,64]{2,1,0:T(8,128)}), f32[27,64,64]{2,1,0:T(8,128)}) %all-reduce.7.cloned.1.call-update) | async-done | bytes 442384 | tf_op jit(solution)/shard_map/psum | solution.py:51
  569.9 2.2 copy.323
  (155 shorter events, 35.9 us)
Async XLA Ops:
  7.2 128.1 %copy-start = (bf16[27,64]{1,0:T(8,128)(2,1)S(1)}, bf16[27,64]{1,0:T(8,128)(2,1)}, u32[]{:S(2)}) copy-start(bf16[27,64]{1,0:T(8,128)(2,1)} %param.13) | copy-start | bytes 10372
  7.2 14.7 %reduce-scatter.4.cloned.1.call-start = ((), (), s32[]{:S(2)}) async-start(), calls=%async_computation.7 | async-start | bytes 393216 | tf_op jit(solution)/shard_map/reduce_scatter | solution.py:71
  11.4 22.3 %reduce-scatter.6.cloned.1.call-start = ((), (), s32[]{:S(2)}) async-start(), calls=%async_computation.8 | async-start | bytes 393216 | tf_op jit(solution)/shard_map/reduce_scatter | solution.py:72
  23.8 13.2 %all-to-all-start = ((f32[8,1,4096]{2,1,0:T(1,128)}), f32[8,1,4096]{2,1,0:T(1,128)S(1)}, u32[]{:S(2)}, u32[]{:S(2)}) async-start(f32[8,1,4096]{2,1,0:T(1,128)} %reshape.165), calls=%async_computation.1 | async-start | bytes 262144 | tf_op jit(solution)/shard_map/all_to_all | solution.py:77
  37.0 12.0 %all-to-all-start.1 = ((f32[8,1,4096]{2,1,0:T(1,128)}), f32[8,1,4096]{2,1,0:T(1,128)S(1)}, u32[]{:S(2)}, u32[]{:S(2)}) async-start(f32[8,1,4096]{2,1,0:T(1,128)} %reshape.167), calls=%async_computation.3 | async-start | bytes 262144 | tf_op jit(solution)/shard_map/all_to_all | solution.py:84
  48.2 6.9 %copy-start.30 = (f32[32,512]{1,0:T(8,128)S(1)}, f32[32,512]{1,0:T(8,128)}, u32[]{:S(2)}) copy-start(f32[32,512]{1,0:T(8,128)} %param.9) | copy-start | bytes 196612
  80.7 12.6 %all-to-all-start.2 = ((f32[8,1,4096]{2,1,0:T(1,128)}), f32[8,1,4096]{2,1,0:T(1,128)S(1)}, u32[]{:S(2)}, u32[]{:S(2)}) async-start(f32[8,1,4096]{2,1,0:T(1,128)} %reshape.169), calls=%async_computation.4 | async-start | bytes 262144 | tf_op jit(solution)/shard_map/all_to_all | solution.py:109
  93.2 11.8 %all-to-all-start.3 = ((f32[8,1,4096]{2,1,0:T(1,128)}), f32[8,1,4096]{2,1,0:T(1,128)S(1)}, u32[]{:S(2)}, u32[]{:S(2)}) async-start(f32[8,1,4096]{2,1,0:T(1,128)} %reshape.171), calls=%async_computation.5 | async-start | bytes 262144 | tf_op jit(solution)/shard_map/all_to_all | solution.py:116
  97.7 19.8 %reduce-scatter.8.cloned.1.call-start = ((), (), s32[]{:S(2)}) async-start(), calls=%async_computation.9 | async-start | bytes 393216 | tf_op jit(solution)/shard_map/reduce_scatter | solution.py:131
  111.9 377.2 %all-reduce.5.cloned.1.call-start = ((), (), s32[]{:S(2)}) async-start(), calls=%async_computation.10 | async-start | bytes 1769472 | tf_op jit(solution)/shard_map/psum | solution.py:51
  117.5 17.8 %copy-start.28 = (bf16[64,2,64,256]{3,2,1,0:T(8,128)(2,1)S(1)}, bf16[64,2,64,256]{3,2,1,0:T(8,128)(2,1)}, u32[]{:S(2)}) copy-start(bf16[64,2,64,256]{3,2,1,0:T(8,128)(2,1)} %param.11) | copy-start | bytes 12582916
  118.6 5.0 collective-permute-start
  122.4 5.5 collective-permute-start.1
  127.9 2.6 collective-permute-start.2
  129.2 3.1 collective-permute-start.3
  139.8 2.0 copy-start.2
  141.8 52.0 %collective-permute-start.4 = (bf16[64,2,1,256]{3,0,2,1:T(8,128)(2,1)S(1)}, bf16[64,2,1,256]{3,0,2,1:T(8,128)(2,1)S(1)}, u32[]{:S(2)}, u32[]{:S(2)}) collective-permute-start(bf16[64,2,1,256]{3,0,2,1:T(8,128)(2,1)S(1)} %get-tuple-element.42), channel_id=1, source_target_pairs={{0,2},{2,4},{4,6},{6,8},{8,10},{10,12},{12,14},{1,3},{3,5},{5,7},{... | collective-permute-start | bytes 196616 | tf_op jit(solution)/shard_map/ppermute | solution.py:18
  146.1 47.7 %collective-permute-start.5 = (bf16[64,2,1,256]{3,0,2,1:T(8,128)(2,1)S(1)}, bf16[64,2,1,256]{3,0,2,1:T(8,128)(2,1)S(1)}, u32[]{:S(2)}, u32[]{:S(2)}) collective-permute-start(bf16[64,2,1,256]{3,0,2,1:T(8,128)(2,1)S(1)} %get-tuple-element.43), channel_id=1, source_target_pairs={{2,0},{4,2},{6,4},{8,6},{10,8},{12,10},{14,12},{3,1},{5,3},{7,5},{... | collective-permute-start | bytes 196616 | tf_op jit(solution)/shard_map/ppermute | solution.py:19
  202.4 11.3 %collective-permute-start.6 = (bf16[64,2,66,1]{2,0,3,1:T(8,128)(2,1)S(1)}, bf16[64,2,66,1]{2,0,3,1:T(8,128)(2,1)S(1)}, u32[]{:S(2)}, u32[]{:S(2)}) collective-permute-start(bf16[64,2,66,1]{2,0,3,1:T(8,128)(2,1)S(1)} %copy.101), channel_id=1, source_target_pairs={{0,1},{2,3},{4,5},{6,7},{8,9},{10,11},{12,13},{14,15},{16,17},{18,... | collective-permute-start | bytes 50696 | tf_op jit(solution)/shard_map/ppermute | solution.py:18
  206.2 12.0 %collective-permute-start.7 = (bf16[64,2,66,1]{2,0,3,1:T(8,128)(2,1)S(1)}, bf16[64,2,66,1]{2,0,3,1:T(8,128)(2,1)S(1)}, u32[]{:S(2)}, u32[]{:S(2)}) collective-permute-start(bf16[64,2,66,1]{2,0,3,1:T(8,128)(2,1)S(1)} %copy.102), channel_id=1, source_target_pairs={{1,0},{3,2},{5,4},{7,6},{9,8},{11,10},{13,12},{15,14},{17,16},{19,... | collective-permute-start | bytes 50696 | tf_op jit(solution)/shard_map/ppermute | solution.py:19
  230.9 9.2 %copy-start.3 = (bf16[64,2,64,256]{3,0,2,1:T(8,128)(2,1)S(1)}, bf16[64,2,64,256]{3,0,2,1:T(8,128)(2,1)}, u32[]{:S(2)}) copy-start(bf16[64,2,64,256]{3,0,2,1:T(8,128)(2,1)} %copy-done.2) | copy-start | bytes 12582916
  230.9 9.2 %copy-start.4 = (bf16[64,2,66,1]{3,0,2,1:T(8,128)(2,1)S(1)}, bf16[64,2,66,1]{3,0,2,1:T(8,128)(2,1)}, u32[]{:S(2)}) copy-start(bf16[64,2,66,1]{3,0,2,1:T(8,128)(2,1)} %copy.103) | copy-start | bytes 50692
  313.1 14.6 %copy-start.29 = (bf16[27,64,64]{2,1,0:T(8,128)(2,1)S(1)}, bf16[27,64,64]{2,1,0:T(8,128)(2,1)}, u32[]{:S(2)}) copy-start(bf16[27,64,64]{2,1,0:T(8,128)(2,1)} %param.12) | copy-start | bytes 663556
  327.7 8.5 %copy-start.10 = (bf16[1,64,2,64,256]{4,1,3,2,0:T(8,128)(2,1)S(1)}, bf16[1,64,2,64,256]{4,1,3,2,0:T(8,128)(2,1)}, u32[]{:S(2)}) copy-start(bf16[1,64,2,64,256]{4,1,3,2,0:T(8,128)(2,1)} %get-tuple-element.40) | copy-start | bytes 12582916
  327.7 10.0 %copy-start.21 = (bf16[1,64,2,64,256]{4,1,3,2,0:T(8,128)(2,1)S(1)}, bf16[1,64,2,64,256]{4,1,3,2,0:T(8,128)(2,1)}, u32[]{:S(2)}) copy-start(bf16[1,64,2,64,256]{4,1,3,2,0:T(8,128)(2,1)} %get-tuple-element.26) | copy-start | bytes 12582916
  327.7 11.2 %copy-start.22 = (bf16[1,64,2,64,256]{4,1,3,2,0:T(8,128)(2,1)S(1)}, bf16[1,64,2,64,256]{4,1,3,2,0:T(8,128)(2,1)}, u32[]{:S(2)}) copy-start(bf16[1,64,2,64,256]{4,1,3,2,0:T(8,128)(2,1)} %get-tuple-element.27) | copy-start | bytes 12582916
  354.2 6.9 %copy-start.19 = (bf16[1,64,2,64,256]{4,1,3,2,0:T(8,128)(2,1)S(1)}, bf16[1,64,2,64,256]{4,1,3,2,0:T(8,128)(2,1)}, u32[]{:S(2)}) copy-start(bf16[1,64,2,64,256]{4,1,3,2,0:T(8,128)(2,1)} %get-tuple-element.24) | copy-start | bytes 12582916
  354.2 7.5 %copy-start.20 = (bf16[1,64,2,64,256]{4,1,3,2,0:T(8,128)(2,1)S(1)}, bf16[1,64,2,64,256]{4,1,3,2,0:T(8,128)(2,1)}, u32[]{:S(2)}) copy-start(bf16[1,64,2,64,256]{4,1,3,2,0:T(8,128)(2,1)} %get-tuple-element.25) | copy-start | bytes 12582916
  359.1 2.0 copy-start.26
  366.9 11.4 %copy-start.17 = (bf16[1,64,2,64,256]{4,1,3,2,0:T(8,128)(2,1)S(1)}, bf16[1,64,2,64,256]{4,1,3,2,0:T(8,128)(2,1)}, u32[]{:S(2)}) copy-start(bf16[1,64,2,64,256]{4,1,3,2,0:T(8,128)(2,1)} %get-tuple-element.22) | copy-start | bytes 12582916
  366.9 11.4 %copy-start.18 = (bf16[1,64,2,64,256]{4,1,3,2,0:T(8,128)(2,1)S(1)}, bf16[1,64,2,64,256]{4,1,3,2,0:T(8,128)(2,1)}, u32[]{:S(2)}) copy-start(bf16[1,64,2,64,256]{4,1,3,2,0:T(8,128)(2,1)} %get-tuple-element.23) | copy-start | bytes 12582916
  385.2 11.5 %copy-start.15 = (bf16[1,64,2,64,256]{4,1,3,2,0:T(8,128)(2,1)S(1)}, bf16[1,64,2,64,256]{4,1,3,2,0:T(8,128)(2,1)}, u32[]{:S(2)}) copy-start(bf16[1,64,2,64,256]{4,1,3,2,0:T(8,128)(2,1)} %get-tuple-element.20) | copy-start | bytes 12582916
  385.2 11.5 %copy-start.16 = (bf16[1,64,2,64,256]{4,1,3,2,0:T(8,128)(2,1)S(1)}, bf16[1,64,2,64,256]{4,1,3,2,0:T(8,128)(2,1)}, u32[]{:S(2)}) copy-start(bf16[1,64,2,64,256]{4,1,3,2,0:T(8,128)(2,1)} %get-tuple-element.21) | copy-start | bytes 12582916
  402.0 11.3 %copy-start.13 = (bf16[1,64,2,64,256]{4,1,3,2,0:T(8,128)(2,1)S(1)}, bf16[1,64,2,64,256]{4,1,3,2,0:T(8,128)(2,1)}, u32[]{:S(2)}) copy-start(bf16[1,64,2,64,256]{4,1,3,2,0:T(8,128)(2,1)} %get-tuple-element.18) | copy-start | bytes 12582916
  402.0 11.3 %copy-start.14 = (bf16[1,64,2,64,256]{4,1,3,2,0:T(8,128)(2,1)S(1)}, bf16[1,64,2,64,256]{4,1,3,2,0:T(8,128)(2,1)}, u32[]{:S(2)}) copy-start(bf16[1,64,2,64,256]{4,1,3,2,0:T(8,128)(2,1)} %get-tuple-element.19) | copy-start | bytes 12582916
  412.3 0.9 copy-start.27
  419.9 10.5 %copy-start.11 = (bf16[1,64,2,64,256]{4,1,3,2,0:T(8,128)(2,1)S(1)}, bf16[1,64,2,64,256]{4,1,3,2,0:T(8,128)(2,1)}, u32[]{:S(2)}) copy-start(bf16[1,64,2,64,256]{4,1,3,2,0:T(8,128)(2,1)} %get-tuple-element.16) | copy-start | bytes 12582916
  419.9 10.4 %copy-start.12 = (bf16[1,64,2,64,256]{4,1,3,2,0:T(8,128)(2,1)S(1)}, bf16[1,64,2,64,256]{4,1,3,2,0:T(8,128)(2,1)}, u32[]{:S(2)}) copy-start(bf16[1,64,2,64,256]{4,1,3,2,0:T(8,128)(2,1)} %get-tuple-element.17) | copy-start | bytes 12582916
  419.9 10.4 %copy-start.23 = (bf16[1,64,2,64,256]{4,1,3,2,0:T(8,128)(2,1)S(1)}, bf16[1,64,2,64,256]{4,1,3,2,0:T(8,128)(2,1)}, u32[]{:S(2)}) copy-start(bf16[1,64,2,64,256]{4,1,3,2,0:T(8,128)(2,1)} %get-tuple-element.31) | copy-start | bytes 12582916
  430.3 5.3 copy-start.24
  435.7 9.4 %copy-start.5 = (bf16[1,64,2,64,256]{4,1,3,2,0:T(8,128)(2,1)S(1)}, bf16[1,64,2,64,256]{4,1,3,2,0:T(8,128)(2,1)}, u32[]{:S(2)}) copy-start(bf16[1,64,2,64,256]{4,1,3,2,0:T(8,128)(2,1)} %get-tuple-element.41) | copy-start | bytes 12582916
  435.7 9.4 %copy-start.8 = (bf16[1,64,2,64,256]{4,1,3,2,0:T(8,128)(2,1)S(1)}, bf16[1,64,2,64,256]{4,1,3,2,0:T(8,128)(2,1)}, u32[]{:S(2)}) copy-start(bf16[1,64,2,64,256]{4,1,3,2,0:T(8,128)(2,1)} %get-tuple-element.14) | copy-start | bytes 12582916
  435.7 9.4 %copy-start.9 = (bf16[1,64,2,64,256]{4,1,3,2,0:T(8,128)(2,1)S(1)}, bf16[1,64,2,64,256]{4,1,3,2,0:T(8,128)(2,1)}, u32[]{:S(2)}) copy-start(bf16[1,64,2,64,256]{4,1,3,2,0:T(8,128)(2,1)} %get-tuple-element.15) | copy-start | bytes 12582916
  450.5 9.4 %copy-start.6 = (bf16[1,64,2,64,256]{4,1,3,2,0:T(8,128)(2,1)S(1)}, bf16[1,64,2,64,256]{4,1,3,2,0:T(8,128)(2,1)}, u32[]{:S(2)}) copy-start(bf16[1,64,2,64,256]{4,1,3,2,0:T(8,128)(2,1)} %get-tuple-element.13) | copy-start | bytes 12582916
  450.5 9.4 %copy-start.7 = (bf16[1,64,2,64,256]{4,1,3,2,0:T(8,128)(2,1)S(1)}, bf16[1,64,2,64,256]{4,1,3,2,0:T(8,128)(2,1)}, u32[]{:S(2)}) copy-start(bf16[1,64,2,64,256]{4,1,3,2,0:T(8,128)(2,1)} %get-tuple-element.29) | copy-start | bytes 12582916
  450.5 9.4 %copy-start.25 = (bf16[1,64,2,64,256]{4,1,3,2,0:T(8,128)(2,1)S(1)}, bf16[1,64,2,64,256]{4,1,3,2,0:T(8,128)(2,1)}, u32[]{:S(2)}) copy-start(bf16[1,64,2,64,256]{4,1,3,2,0:T(8,128)(2,1)} %get-tuple-element.34) | copy-start | bytes 12582916
  471.6 98.2 %all-reduce.7.cloned.1.call-start = ((), (), s32[]{:S(2)}) async-start(), calls=%async_computation.11 | async-start | bytes 1769472 | tf_op jit(solution)/shard_map/psum | solution.py:51
  489.2 82.9 %copy-start.1 = (bf16[27,64]{1,0:T(8,128)(2,1)S(1)}, bf16[27,64]{1,0:T(8,128)(2,1)}, u32[]{:S(2)}) copy-start(bf16[27,64]{1,0:T(8,128)(2,1)} %param.13) | copy-start | bytes 10372
Sparse Core Ops, SparseCore 0:
  11.5 10.3 reduce-scatter.3
  24.8 8.8 reduce-scatter.5
  112.0 5.4 reduce-scatter.7
  471.8 17.3 all-reduce.4
  492.8 76.9 all-reduce.6
